TPU v7x, 32 devices: a whole 2x2x4 slice. The times are simulated.
32 devices in a mesh: row: 8 (over y, x, core), col: 4 (over z).
Axes of the slice: x: 2, y: 2, z: 4, core: 2. Of those that a mesh axis runs over, the one named last changes fastest.
Arguments:
- left_factors: float32 [128, 256, 32], P(None, ('row', 'col')), may hold values from -12 to 12
- right_factors: float32 [128, 128, 32], P(None, ('col', 'row')), may hold values from -12 to 12
- weight: float32 [1024, 128], replicated, may hold values from -0.1875 to 0.1875
- bias: float32 [128], replicated, may hold values from -2 to 2
- cotangent: float32 [256, 128, 128], P('row', 'col'), may hold values from -6 to 6
Outputs:
- pair_out: float32 [256, 128, 128], P('row', 'col')
- left_grad: float32 [128, 256, 32], P(None, ('row', 'col'))
- right_grad: float32 [128, 128, 32], P(None, ('col', 'row'))
- weight_grad: float32 [1024, 128], replicated
- bias_grad: float32 [128], replicated
All inputs are finite; a program needn't handle non-finite values.
Results may differ from a plain program's by a relative error of at most 0.0001.
Values sent between devices are 32-bit elements; how exact they have to be, the bound alone decides.
A program may use at most 64 MiB of HBM per device.

v0:
```python
import jax
import jax.numpy as jnp
from jax import lax
from jax.sharding import PartitionSpec as P


def per_device(left_factors, right_factors, weight, bias, cotangent):
    high = lax.Precision.HIGHEST
    samples = left_factors.shape[0]
    width = left_factors.shape[2]
    pair_width = weight.shape[1]
    left_all = lax.all_gather(left_factors, "col", axis=1, tiled=True)
    right_all = lax.all_gather(right_factors, "row", axis=1, tiled=True)
    tile_rows = left_all.shape[1]
    tile_cols = right_all.shape[1]
    step_rows = 16
    blocks = tile_rows // step_rows
    left_blocks = left_all.reshape(samples, blocks, step_rows, width).transpose(1, 0, 2, 3)
    cot_blocks = cotangent.reshape(blocks, step_rows, tile_cols, pair_width)

    def visit(carry, item):
        weight_sum, right_sum = carry
        left_block, cot_block = item
        outer = jnp.einsum("sic,sjd->ijcd", left_block, right_all, precision=high) / samples
        flat = outer.reshape(step_rows, tile_cols, width * width)
        pair_block = jnp.einsum("ijk,ke->ije", flat, weight, precision=high) + bias
        grad_flat = jnp.einsum("ije,ke->ijk", cot_block, weight, precision=high)
        weight_sum = weight_sum + jnp.einsum("ijk,ije->ke", flat, cot_block, precision=high)
        grad_outer = grad_flat.reshape(step_rows, tile_cols, width, width)
        left_block_grad = (
            jnp.einsum("ijcd,sjd->sic", grad_outer, right_all, precision=high) / samples
        )
        right_sum = (
            right_sum
            + jnp.einsum("ijcd,sic->sjd", grad_outer, left_block, precision=high) / samples
        )
        return ((weight_sum, right_sum), (pair_block, left_block_grad))

    start = (
        jnp.zeros((width * width, pair_width), jnp.float32),
        jnp.zeros((samples, tile_cols, width), jnp.float32),
    )
    (weight_part, right_part), (pair_blocks, left_pieces) = lax.scan(
        visit, start, (left_blocks, cot_blocks)
    )
    pair_out = pair_blocks.reshape(tile_rows, tile_cols, pair_width)
    left_part = left_pieces.transpose(1, 0, 2, 3).reshape(samples, tile_rows, width)
    bias_part = jnp.sum(cotangent, axis=(0, 1))
    left_total = lax.psum(left_part, "col")
    right_total = lax.psum(right_part, "row")
    left_share = tile_rows // lax.axis_size("col")
    right_share = tile_cols // lax.axis_size("row")
    left_grad = lax.dynamic_slice_in_dim(
        left_total, lax.axis_index("col") * left_share, left_share, 1
    )
    right_grad = lax.dynamic_slice_in_dim(
        right_total, lax.axis_index("row") * right_share, right_share, 1
    )
    weight_half, bias_half = lax.psum((weight_part, bias_part), "col")
    weight_total, bias_total = lax.psum((weight_half, bias_half), "row")
    total_rows = tile_rows * lax.axis_size("row")
    weight_grad = weight_total / total_rows
    bias_grad = bias_total / total_rows
    return (pair_out, left_grad, right_grad, weight_grad, bias_grad)


def solution(mesh):
    in_specs = (
        P(None, ("row", "col"), None),
        P(None, ("col", "row"), None),
        P(),
        P(),
        P("row", "col", None),
    )
    out_specs = (
        P("row", "col", None),
        P(None, ("row", "col"), None),
        P(None, ("col", "row"), None),
        P(),
        P(),
    )
    return jax.shard_map(
        per_device, mesh=mesh, in_specs=in_specs, out_specs=out_specs, check_vma=False
    )
```

profile of v0, /device:TPU:0, one launch (start us, length us, event | category | flops | bytes accessed | tf_op | source)
XLA Modules:
  0.0 329.0 jit_solution(1549016555022079670)
XLA Ops:
  7.2 11.6 %all_gather.7 = f32[128,32,32]{0,2,1:T(8,128)S(1)} all-gather(f32[128,4,32]{0,2,1:T(8,128)} %param.8), channel_id=1, replica_groups=mesh['row'=8,'col'=4] {'row'}, dimensions={1}, use_global_device_ids=true | all-gather | bytes 589824 | tf_op jit(solution)/shard_map/all_gather | solution.py:13
  19.2 16.6 %all_gather.6 = f32[128,32,32]{0,2,1:T(8,128)S(1)} all-gather(f32[128,8,32]{0,2,1:T(8,128)} %param.7), channel_id=1, replica_groups=mesh['row'=8,'col'=4] {'col'}, dimensions={1}, use_global_device_ids=true | all-gather | bytes 655360 | tf_op jit(solution)/shard_map/all_gather | solution.py:12
  35.7 170.8 %while.17 = (s32[]{:T(128)}, f32[1024,128]{1,0:T(8,128)}, f32[128,32,32]{0,2,1:T(8,128)}, f32[2,16,32,128]{3,2,1,0:T(8,128)}, f32[2,128,16,32]{1,3,2,0:T(8,128)}...) while((s32[]{:T(128)}, f32[1024,128]{1,0:T(8,128)}, ...), condition=%wide.region_1.2_spmd.clone, body=%wide.region_0.1_spmd.clone.sunk | while | flops 4833148928 | bytes 49812356 | solution.py:43
  59.9 9.1 %multiply_bitcast_fusion.2 = f32[16,32,32,32]{3,2,1,0:T(8,128)} fusion(f32[128,32,32]{0,1,2:T(8,128)S(1)} %get-tuple-element.222, f32[2,128,16,32]{1,3,2,0:T(8,128)S(1)} %get-tuple-element.221, s32[]{:T(128)} %get-tuple-element.204), kind=kOutput, calls=%fused_computation.2.clone.1 | convolution fusion | flops 805830656 | bytes 2883588 | tf_op jit(solution)/shard_map/while/body/eval_jaxpr/sic,sjd->ijcd/dot_general | solution.py:24
  68.9 6.7 %reshape.43 = f32[16,32,1024]{2,1,0:T(8,128)S(1)} reshape(f32[16,32,32,32]{3,2,1,0:T(8,128)} %multiply_bitcast_fusion.2) | data formatting | bytes 4194304 | tf_op jit(solution)/shard_map/while/body/eval_jaxpr/reshape | solution.py:25
  75.7 5.2 %fusion.67 = f32[1024,128]{1,0:T(8,128)} fusion(f32[16,32,1024]{2,1,0:T(8,128)S(1)} %reshape.43, f32[1024,128]{1,0:T(8,128)} %get-tuple-element.205, pred[]{:T(512)S(6)} %compare.3, f32[2,16,32,128]{3,2,1,0:T(8,128)} %get-tuple-element.223, s32[]{:T(128)} %get-tuple-element.204), kind=kOutput, calls=%fused_computation.5.clone.1 | convolution fusion | flops 805568512 | bytes 3408385 | tf_op jit(solution)/shard_map/while/body/eval_jaxpr/ijk,ije->ke/dot_general | solution.py:28
  80.9 7.7 %fusion.68 = f32[16,32,32,32]{3,1,2,0:T(8,128)S(1)} fusion(f32[32,32,128,1]{2,1,0,3:T(8,128)S(1)} %bitcast.110, f32[2,16,32,128]{3,2,1,0:T(8,128)} %get-tuple-element.223, s32[]{:T(128)} %get-tuple-element.204), kind=kOutput, calls=%fused_computation.19.clone.1 | convolution fusion | flops 805306368 | bytes 2884096 | tf_op jit(solution)/shard_map/while/body/eval_jaxpr/ije,ke->ijk/dot_general | solution.py:27
  88.6 3.2 copy-done
  91.8 17.0 %fusion.69 = f32[128,32,32]{0,2,1:T(8,128)S(1)} fusion(f32[16,32,32,32]{3,1,2,0:T(8,128)S(1)} %fusion.68, f32[128,32,32]{0,2,1:T(8,128)S(1)} %copy-done.4, pred[]{:T(512)S(6)} %compare.3, f32[2,128,16,32]{1,3,2,0:T(8,128)} %copy-done.2, s32[]{:T(128)} %get-tuple-element.204), kind=kOutput, calls=%fused_computation.7.clone.1 | convolution fusion | flops 805699584 | bytes 3408385 | tf_op jit(solution)/shard_map/while/body/eval_jaxpr/ijcd,sic->sjd/dot_general | solution.py:35
  109.6 2.5 fusion.70
  112.1 10.6 %copy.39 = f32[16,32,32,32]{1,2,3,0:T(8,128)} copy(f32[16,32,32,32]{3,1,2,0:T(8,128)} %copy-done) | data formatting | bytes 4194304 | tf_op jit(solution)/shard_map/while/body/eval_jaxpr/ije,ke->ijk/dot_general | solution.py:27
  122.7 9.2 %fusion.71 = f32[2,128,16,32]{1,3,2,0:T(8,128)S(1)} fusion(f32[2,128,16,32]{1,3,2,0:T(8,128)S(1)} %copy-done.6, s32[]{:T(128)} %get-tuple-element.204, f32[16,32,32,32]{1,2,3,0:T(8,128)} %copy.39, f32[128,32,32]{0,1,2:T(8,128)S(1)} %get-tuple-element.222), kind=kOutput, calls=%fused_computation.14.clone.1 | convolution fusion | flops 805371904 | bytes 2883588 | tf_op jit(solution)/shard_map/while/body/eval_jaxpr/ijcd,sjd->sic/dot_general | solution.py:31
  133.5 9.0 %multiply_bitcast_fusion.2 = f32[16,32,32,32]{3,2,1,0:T(8,128)} fusion(f32[128,32,32]{0,1,2:T(8,128)S(1)} %get-tuple-element.222, f32[2,128,16,32]{1,3,2,0:T(8,128)S(1)} %get-tuple-element.221, s32[]{:T(128)} %get-tuple-element.204), kind=kOutput, calls=%fused_computation.2.clone.1 | convolution fusion | flops 805830656 | bytes 2883588 | tf_op jit(solution)/shard_map/while/body/eval_jaxpr/sic,sjd->ijcd/dot_general | solution.py:24
  142.6 6.7 %reshape.43 = f32[16,32,1024]{2,1,0:T(8,128)S(1)} reshape(f32[16,32,32,32]{3,2,1,0:T(8,128)} %multiply_bitcast_fusion.2) | data formatting | bytes 4194304 | tf_op jit(solution)/shard_map/while/body/eval_jaxpr/reshape | solution.py:25
  149.3 5.4 %fusion.67 = f32[1024,128]{1,0:T(8,128)} fusion(f32[16,32,1024]{2,1,0:T(8,128)S(1)} %reshape.43, f32[1024,128]{1,0:T(8,128)} %get-tuple-element.205, pred[]{:T(512)S(6)} %compare.3, f32[2,16,32,128]{3,2,1,0:T(8,128)} %get-tuple-element.223, s32[]{:T(128)} %get-tuple-element.204), kind=kOutput, calls=%fused_computation.5.clone.1 | convolution fusion | flops 805568512 | bytes 3408385 | tf_op jit(solution)/shard_map/while/body/eval_jaxpr/ijk,ije->ke/dot_general | solution.py:28
  154.7 7.7 %fusion.68 = f32[16,32,32,32]{3,1,2,0:T(8,128)S(1)} fusion(f32[32,32,128,1]{2,1,0,3:T(8,128)S(1)} %bitcast.110, f32[2,16,32,128]{3,2,1,0:T(8,128)} %get-tuple-element.223, s32[]{:T(128)} %get-tuple-element.204), kind=kOutput, calls=%fused_computation.19.clone.1 | convolution fusion | flops 805306368 | bytes 2884096 | tf_op jit(solution)/shard_map/while/body/eval_jaxpr/ije,ke->ijk/dot_general | solution.py:27
  162.4 3.2 copy-done
  165.6 17.0 %fusion.69 = f32[128,32,32]{0,2,1:T(8,128)S(1)} fusion(f32[16,32,32,32]{3,1,2,0:T(8,128)S(1)} %fusion.68, f32[128,32,32]{0,2,1:T(8,128)S(1)} %copy-done.4, pred[]{:T(512)S(6)} %compare.3, f32[2,128,16,32]{1,3,2,0:T(8,128)} %copy-done.2, s32[]{:T(128)} %get-tuple-element.204), kind=kOutput, calls=%fused_computation.7.clone.1 | convolution fusion | flops 805699584 | bytes 3408385 | tf_op jit(solution)/shard_map/while/body/eval_jaxpr/ijcd,sic->sjd/dot_general | solution.py:35
  185.9 10.6 %copy.39 = f32[16,32,32,32]{1,2,3,0:T(8,128)} copy(f32[16,32,32,32]{3,1,2,0:T(8,128)} %copy-done) | data formatting | bytes 4194304 | tf_op jit(solution)/shard_map/while/body/eval_jaxpr/ije,ke->ijk/dot_general | solution.py:27
  196.5 9.2 %fusion.71 = f32[2,128,16,32]{1,3,2,0:T(8,128)S(1)} fusion(f32[2,128,16,32]{1,3,2,0:T(8,128)S(1)} %copy-done.6, s32[]{:T(128)} %get-tuple-element.204, f32[16,32,32,32]{1,2,3,0:T(8,128)} %copy.39, f32[128,32,32]{0,1,2:T(8,128)S(1)} %get-tuple-element.222), kind=kOutput, calls=%fused_computation.14.clone.1 | convolution fusion | flops 805371904 | bytes 2883588 | tf_op jit(solution)/shard_map/while/body/eval_jaxpr/ijcd,sjd->sic/dot_general | solution.py:31
  206.6 52.6 %all-reduce.7.cloned.1.call-done = (f32[128,32,32]{0,2,1:T(8,128)}, f32[1024,128]{1,0:T(8,128)}) async-done(((f32[128,32,32]{0,2,1:T(8,128)}, f32[1024,128]{1,0:T(8,128)}), (f32[128,32,32]{0,2,1:T(8,128)}, f32[1024,128]{1,0:T(8,128)})) %all-reduce.7.cloned.1.call-update) | async-done | bytes 1048592 | tf_op jit(solution)/shard_map/psum | solution.py:49
  260.4 10.0 %psum.46 = f32[128]{0:T(128)S(1)} all-reduce(f32[128]{0:T(128)S(1)} %reduce_sum.9), channel_id=1, replica_groups=mesh['row'=8,'col'=4] {'col'}, use_global_device_ids=true, to_apply=%region_7.8 | all-reduce | flops 128 | bytes 1024 | tf_op jit(solution)/shard_map/psum | solution.py:59
  270.4 11.8 %psum.47 = f32[128]{0:T(128)S(1)} all-reduce(f32[128]{0:T(128)S(1)} %psum.46), channel_id=1, replica_groups=mesh['row'=8,'col'=4] {'row'}, use_global_device_ids=true, to_apply=%region_8.9 | all-reduce | flops 128 | bytes 1024 | tf_op jit(solution)/shard_map/psum | solution.py:60
  284.4 34.1 %all-reduce.5.cloned.1.call-done = (f32[128,32,32]{0,2,1:T(8,128)}, f32[1024,128]{1,0:T(8,128)}) async-done(((f32[128,32,32]{0,2,1:T(8,128)}, f32[1024,128]{1,0:T(8,128)}), (f32[128,32,32]{0,2,1:T(8,128)}, f32[1024,128]{1,0:T(8,128)})) %all-reduce.5.cloned.1.call-update) | async-done | bytes 1048592 | tf_op jit(solution)/shard_map/psum | solution.py:50
  (49 shorter events, 14.3 us)
Async XLA Ops:
  7.2 252.0 %all-reduce.7.cloned.1.call-start = ((), (), s32[]{:S(2)}) async-start(), calls=%async_computation.1 | async-start | bytes 2097152 | tf_op jit(solution)/shard_map/psum | solution.py:49
  59.1 0.8 copy-start.2
  68.9 12.0 %copy-start.1 = (f32[1024,128]{1,0:T(8,128)S(1)}, f32[1024,128]{1,0:T(8,128)}, u32[]{:S(2)}) copy-start(f32[1024,128]{1,0:T(8,128)} %get-tuple-element.224) | copy-start | bytes 1572868 | tf_op jit(solution)/shard_map/while
  75.6 16.1 %copy-start.4 = (f32[128,32,32]{0,2,1:T(8,128)S(1)}, f32[128,32,32]{0,2,1:T(8,128)}, u32[]{:S(2)}) copy-start(f32[128,32,32]{0,2,1:T(8,128)} %get-tuple-element.206) | copy-start | bytes 1572868 | tf_op jit(solution)/shard_map/while
  80.9 28.7 %copy-start.8 = (f32[128]{0:T(128)S(1)}, f32[128]{0:T(128)}, u32[]{:S(2)}) copy-start(f32[128]{0:T(128)} %get-tuple-element.225) | copy-start | bytes 1540 | tf_op jit(solution)/shard_map/while
  88.6 3.2 copy-start
  108.8 0.8 copy-start.5
  112.1 10.6 %copy-start.6 = (f32[2,128,16,32]{1,3,2,0:T(8,128)S(1)}, f32[2,128,16,32]{1,3,2,0:T(8,128)}, u32[]{:S(2)}) copy-start(f32[2,128,16,32]{1,3,2,0:T(8,128)} %get-tuple-element.208) | copy-start | bytes 1572868 | tf_op jit(solution)/shard_map/while
  122.7 10.0 %copy-start.3 = (f32[2,128,16,32]{1,3,2,0:T(8,128)S(1)}, f32[2,128,16,32]{1,3,2,0:T(8,128)}, u32[]{:S(2)}) copy-start(f32[2,128,16,32]{1,3,2,0:T(8,128)} %copy-done.2) | copy-start | bytes 1572868 | tf_op jit(solution)/shard_map/while
  131.9 0.8 copy-start.7
  132.7 0.8 copy-start.2
  142.6 12.1 %copy-start.1 = (f32[1024,128]{1,0:T(8,128)S(1)}, f32[1024,128]{1,0:T(8,128)}, u32[]{:S(2)}) copy-start(f32[1024,128]{1,0:T(8,128)} %get-tuple-element.224) | copy-start | bytes 1572868 | tf_op jit(solution)/shard_map/while
  149.3 16.3 %copy-start.4 = (f32[128,32,32]{0,2,1:T(8,128)S(1)}, f32[128,32,32]{0,2,1:T(8,128)}, u32[]{:S(2)}) copy-start(f32[128,32,32]{0,2,1:T(8,128)} %get-tuple-element.206) | copy-start | bytes 1572868 | tf_op jit(solution)/shard_map/while
  154.7 28.7 %copy-start.8 = (f32[128]{0:T(128)S(1)}, f32[128]{0:T(128)}, u32[]{:S(2)}) copy-start(f32[128]{0:T(128)} %get-tuple-element.225) | copy-start | bytes 1540 | tf_op jit(solution)/shard_map/while
  162.4 3.2 copy-start
  182.6 0.8 copy-start.5
  185.9 10.6 %copy-start.6 = (f32[2,128,16,32]{1,3,2,0:T(8,128)S(1)}, f32[2,128,16,32]{1,3,2,0:T(8,128)}, u32[]{:S(2)}) copy-start(f32[2,128,16,32]{1,3,2,0:T(8,128)} %get-tuple-element.208) | copy-start | bytes 1572868 | tf_op jit(solution)/shard_map/while
  196.5 10.0 %copy-start.3 = (f32[2,128,16,32]{1,3,2,0:T(8,128)S(1)}, f32[2,128,16,32]{1,3,2,0:T(8,128)}, u32[]{:S(2)}) copy-start(f32[2,128,16,32]{1,3,2,0:T(8,128)} %copy-done.2) | copy-start | bytes 1572868 | tf_op jit(solution)/shard_map/while
  205.7 0.8 copy-start.7
  206.6 111.9 %all-reduce.5.cloned.1.call-start = ((), (), s32[]{:S(2)}) async-start(), calls=%async_computation | async-start | bytes 2097152 | tf_op jit(solution)/shard_map/psum | solution.py:50
Sparse Core Ops, SparseCore 0:
  206.7 52.4 all-reduce.6
  262.4 56.0 all-reduce.4
where the time goes:
time: 332 us; the launch traced here: 329 us
  matrix products  101 us (30%)
  waiting for transfers between devices  86.7 us (26%)
  blocking collectives  50 us (15%)
  local copies, waits for them, and re-layouts  49.2 us (15%)
  loops' own time  23.5 us (7%)
  between operations  14.5 us (4%)
  other arithmetic  3.58 us (1%)
    psum x1, waiting for transfers between devices, per_device(): left_total = lax.psum(left_part, 'col')  52.6 us
    psum x1, waiting for transfers between devices, per_device(): right_total = lax.psum(right_part, 'row')  34.1 us
    dot_general x2, matrix products, visit(): jnp.einsum('ijcd,sic->sjd', grad_outer, left_block, precision=high)  33.9 us
    another operation x1, loops' own time, per_device(): lax.scan(visit, start, (left_blocks, cot_blocks))  23.5 us
    dot_general x2, local copies, waits for them, and re-layouts, visit(): grad_flat = jnp.einsum('ije,ke->ijk', cot_block, weight, precision=high)  21.3 us
    dot_general x2, matrix products, visit(): jnp.einsum('ijcd,sjd->sic', grad_outer, right_all, precision=high) / samples  18.4 us
    dot_general x2, matrix products, visit(): jnp.einsum('sic,sjd->ijcd', left_block, right_all, precision=high) / samples  18.1 us
    all_gather x1, blocking collectives, per_device(): left_all = lax.all_gather(left_factors, 'col', axis=1, tiled=True)  16.6 us
  transfers between devices with their start and end apart: 2, of which 2 were waited for; matrix products, arithmetic and copies ran while one was open for 1% of the time, Pallas kernels for 0%

commit v1 on v0

--- a/solution.py
+++ b/solution.py
@@ -46,7 +46,11 @@
     pair_out = pair_blocks.reshape(tile_rows, tile_cols, pair_width)
     left_part = left_pieces.transpose(1, 0, 2, 3).reshape(samples, tile_rows, width)
     bias_part = jnp.sum(cotangent, axis=(0, 1))
-    left_total = lax.psum(left_part, "col")
+    left_total = left_part
+    for hop in (1, 2):
+        left_total = left_total + lax.ppermute(
+            left_total, "col", [(dev, dev ^ hop) for dev in range(4)]
+        )
     right_total = lax.psum(right_part, "row")
     left_share = tile_rows // lax.axis_size("col")
     right_share = tile_cols // lax.axis_size("row")

time: 332 us -> 321 us (0.967)
  waiting for transfers between devices: 86.7 us -> 73.5 us
    psum x1, waiting for transfers between devices: 52.6 us -> 39.1 us  [per_device(): weight_half, bias_half = lax.psum((weight_part, bias_part), 'col')]
  transfers between devices with their start and end apart: 2 -> 4, of which waited for: 2 -> 2; matrix products, arithmetic and copies ran while one was open for 1% -> 2% of each run, Pallas kernels for 0% -> 0%
where the time goes in v1:
time: 321 us; the launch traced here: 319 us
  matrix products  101 us (31%)
  waiting for transfers between devices  73.5 us (23%)
  blocking collectives  50.6 us (16%)
  local copies, waits for them, and re-layouts  47.6 us (15%)
  loops' own time  23.7 us (7%)
  between operations  14.5 us (5%)
  other arithmetic  5.38 us (2%)
    psum x1, waiting for transfers between devices, per_device(): weight_half, bias_half = lax.psum((weight_part, bias_part), 'col')  39.1 us
    psum x1, waiting for transfers between devices, per_device(): right_total = lax.psum(right_part, 'row')  34.4 us
    dot_general x2, matrix products, visit(): jnp.einsum('ijcd,sic->sjd', grad_outer, left_block, precision=high)  33.9 us
    another operation x1, loops' own time, per_device(): lax.scan(visit, start, (left_blocks, cot_blocks))  23.7 us
    dot_general x2, local copies, waits for them, and re-layouts, visit(): grad_flat = jnp.einsum('ije,ke->ijk', cot_block, weight, precision=high)  21.3 us
    dot_general x2, matrix products, visit(): jnp.einsum('ijcd,sjd->sic', grad_outer, right_all, precision=high) / samples  18.4 us
    dot_general x2, matrix products, visit(): jnp.einsum('sic,sjd->ijcd', left_block, right_all, precision=high) / samples  18.1 us
    all_gather x1, blocking collectives, per_device(): left_all = lax.all_gather(left_factors, 'col', axis=1, tiled=True)  16.6 us
  transfers between devices with their start and end apart: 4, of which 2 were waited for; matrix products, arithmetic and copies ran while one was open for 2% of the time, Pallas kernels for 0%

profile of v1, /device:TPU:0, one launch (start us, length us, event | category | flops | bytes accessed | tf_op | source)
XLA Modules:
  0.0 318.9 jit_solution(16383405498086125573)
XLA Ops:
  7.2 11.6 %all_gather.7 = f32[128,32,32]{0,2,1:T(8,128)S(1)} all-gather(f32[128,4,32]{0,2,1:T(8,128)} %param.8), channel_id=1, replica_groups=mesh['row'=8,'col'=4] {'row'}, dimensions={1}, use_global_device_ids=true | all-gather | bytes 589824 | tf_op jit(solution)/shard_map/all_gather | solution.py:13
  19.2 16.6 %all_gather.6 = f32[128,32,32]{0,2,1:T(8,128)S(1)} all-gather(f32[128,8,32]{0,2,1:T(8,128)} %param.7), channel_id=1, replica_groups=mesh['row'=8,'col'=4] {'col'}, dimensions={1}, use_global_device_ids=true | all-gather | bytes 655360 | tf_op jit(solution)/shard_map/all_gather | solution.py:12
  35.7 171.0 %while.17 = (s32[]{:T(128)}, f32[1024,128]{1,0:T(8,128)}, f32[128,32,32]{0,2,1:T(8,128)}, f32[2,16,32,128]{3,2,1,0:T(8,128)}, f32[2,128,16,32]{1,3,2,0:T(8,128)}...) while((s32[]{:T(128)}, f32[1024,128]{1,0:T(8,128)}, ...), condition=%wide.region_1.2_spmd.clone, body=%wide.region_0.1_spmd.clone.sunk | while | flops 4833148928 | bytes 49812356 | solution.py:43
  60.0 9.0 %multiply_bitcast_fusion.2 = f32[16,32,32,32]{3,2,1,0:T(8,128)} fusion(f32[128,32,32]{0,1,2:T(8,128)S(1)} %get-tuple-element.220, f32[2,128,16,32]{1,3,2,0:T(8,128)S(1)} %get-tuple-element.219, s32[]{:T(128)} %get-tuple-element.202), kind=kOutput, calls=%fused_computation.2.clone.1 | convolution fusion | flops 805830656 | bytes 2883588 | tf_op jit(solution)/shard_map/while/body/eval_jaxpr/sic,sjd->ijcd/dot_general | solution.py:24
  69.1 6.7 %reshape.43 = f32[16,32,1024]{2,1,0:T(8,128)S(1)} reshape(f32[16,32,32,32]{3,2,1,0:T(8,128)} %multiply_bitcast_fusion.2) | data formatting | bytes 4194304 | tf_op jit(solution)/shard_map/while/body/eval_jaxpr/reshape | solution.py:25
  75.8 5.2 %fusion.67 = f32[1024,128]{1,0:T(8,128)} fusion(f32[16,32,1024]{2,1,0:T(8,128)S(1)} %reshape.43, f32[1024,128]{1,0:T(8,128)} %get-tuple-element.203, pred[]{:T(512)S(6)} %compare.3, f32[2,16,32,128]{3,2,1,0:T(8,128)} %get-tuple-element.221, s32[]{:T(128)} %get-tuple-element.202), kind=kOutput, calls=%fused_computation.5.clone.1 | convolution fusion | flops 805568512 | bytes 3408385 | tf_op jit(solution)/shard_map/while/body/eval_jaxpr/ijk,ije->ke/dot_general | solution.py:28
  81.1 7.7 %fusion.68 = f32[16,32,32,32]{3,1,2,0:T(8,128)S(1)} fusion(f32[32,32,128,1]{2,1,0,3:T(8,128)S(1)} %bitcast.111, f32[2,16,32,128]{3,2,1,0:T(8,128)} %get-tuple-element.221, s32[]{:T(128)} %get-tuple-element.202), kind=kOutput, calls=%fused_computation.19.clone.1 | convolution fusion | flops 805306368 | bytes 2884096 | tf_op jit(solution)/shard_map/while/body/eval_jaxpr/ije,ke->ijk/dot_general | solution.py:27
  88.7 3.2 %copy-done = f32[16,32,32,32]{3,1,2,0:T(8,128)} copy-done((f32[16,32,32,32]{3,1,2,0:T(8,128)}, f32[16,32,32,32]{3,1,2,0:T(8,128)S(1)}, u32[]{:S(2)}) %copy-start) | copy-done | bytes 2097176 | tf_op jit(solution)/shard_map/while
  91.9 17.0 %fusion.69 = f32[128,32,32]{0,2,1:T(8,128)S(1)} fusion(f32[16,32,32,32]{3,1,2,0:T(8,128)S(1)} %fusion.68, f32[128,32,32]{0,2,1:T(8,128)S(1)} %copy-done.4, pred[]{:T(512)S(6)} %compare.3, f32[2,128,16,32]{1,3,2,0:T(8,128)} %copy-done.2, s32[]{:T(128)} %get-tuple-element.202), kind=kOutput, calls=%fused_computation.7.clone.1 | convolution fusion | flops 805699584 | bytes 3408385 | tf_op jit(solution)/shard_map/while/body/eval_jaxpr/ijcd,sic->sjd/dot_general | solution.py:35
  109.7 2.5 fusion.70
  112.2 10.6 %copy.39 = f32[16,32,32,32]{1,2,3,0:T(8,128)} copy(f32[16,32,32,32]{3,1,2,0:T(8,128)} %copy-done) | data formatting | bytes 4194304 | tf_op jit(solution)/shard_map/while/body/eval_jaxpr/ije,ke->ijk/dot_general | solution.py:27
  122.9 9.2 %fusion.71 = f32[2,128,16,32]{1,3,2,0:T(8,128)S(1)} fusion(f32[2,128,16,32]{1,3,2,0:T(8,128)S(1)} %copy-done.6, s32[]{:T(128)} %get-tuple-element.202, f32[16,32,32,32]{1,2,3,0:T(8,128)} %copy.39, f32[128,32,32]{0,1,2:T(8,128)S(1)} %get-tuple-element.220), kind=kOutput, calls=%fused_computation.14.clone.1 | convolution fusion | flops 805371904 | bytes 2883588 | tf_op jit(solution)/shard_map/while/body/eval_jaxpr/ijcd,sjd->sic/dot_general | solution.py:31
  133.7 9.0 %multiply_bitcast_fusion.2 = f32[16,32,32,32]{3,2,1,0:T(8,128)} fusion(f32[128,32,32]{0,1,2:T(8,128)S(1)} %get-tuple-element.220, f32[2,128,16,32]{1,3,2,0:T(8,128)S(1)} %get-tuple-element.219, s32[]{:T(128)} %get-tuple-element.202), kind=kOutput, calls=%fused_computation.2.clone.1 | convolution fusion | flops 805830656 | bytes 2883588 | tf_op jit(solution)/shard_map/while/body/eval_jaxpr/sic,sjd->ijcd/dot_general | solution.py:24
  142.7 6.7 %reshape.43 = f32[16,32,1024]{2,1,0:T(8,128)S(1)} reshape(f32[16,32,32,32]{3,2,1,0:T(8,128)} %multiply_bitcast_fusion.2) | data formatting | bytes 4194304 | tf_op jit(solution)/shard_map/while/body/eval_jaxpr/reshape | solution.py:25
  149.5 5.4 %fusion.67 = f32[1024,128]{1,0:T(8,128)} fusion(f32[16,32,1024]{2,1,0:T(8,128)S(1)} %reshape.43, f32[1024,128]{1,0:T(8,128)} %get-tuple-element.203, pred[]{:T(512)S(6)} %compare.3, f32[2,16,32,128]{3,2,1,0:T(8,128)} %get-tuple-element.221, s32[]{:T(128)} %get-tuple-element.202), kind=kOutput, calls=%fused_computation.5.clone.1 | convolution fusion | flops 805568512 | bytes 3408385 | tf_op jit(solution)/shard_map/while/body/eval_jaxpr/ijk,ije->ke/dot_general | solution.py:28
  154.9 7.7 %fusion.68 = f32[16,32,32,32]{3,1,2,0:T(8,128)S(1)} fusion(f32[32,32,128,1]{2,1,0,3:T(8,128)S(1)} %bitcast.111, f32[2,16,32,128]{3,2,1,0:T(8,128)} %get-tuple-element.221, s32[]{:T(128)} %get-tuple-element.202), kind=kOutput, calls=%fused_computation.19.clone.1 | convolution fusion | flops 805306368 | bytes 2884096 | tf_op jit(solution)/shard_map/while/body/eval_jaxpr/ije,ke->ijk/dot_general | solution.py:27
  162.5 3.2 %copy-done = f32[16,32,32,32]{3,1,2,0:T(8,128)} copy-done((f32[16,32,32,32]{3,1,2,0:T(8,128)}, f32[16,32,32,32]{3,1,2,0:T(8,128)S(1)}, u32[]{:S(2)}) %copy-start) | copy-done | bytes 2097176 | tf_op jit(solution)/shard_map/while
  165.8 17.0 %fusion.69 = f32[128,32,32]{0,2,1:T(8,128)S(1)} fusion(f32[16,32,32,32]{3,1,2,0:T(8,128)S(1)} %fusion.68, f32[128,32,32]{0,2,1:T(8,128)S(1)} %copy-done.4, pred[]{:T(512)S(6)} %compare.3, f32[2,128,16,32]{1,3,2,0:T(8,128)} %copy-done.2, s32[]{:T(128)} %get-tuple-element.202), kind=kOutput, calls=%fused_computation.7.clone.1 | convolution fusion | flops 805699584 | bytes 3408385 | tf_op jit(solution)/shard_map/while/body/eval_jaxpr/ijcd,sic->sjd/dot_general | solution.py:35
  186.0 10.6 %copy.39 = f32[16,32,32,32]{1,2,3,0:T(8,128)} copy(f32[16,32,32,32]{3,1,2,0:T(8,128)} %copy-done) | data formatting | bytes 4194304 | tf_op jit(solution)/shard_map/while/body/eval_jaxpr/ije,ke->ijk/dot_general | solution.py:27
  196.7 9.2 %fusion.71 = f32[2,128,16,32]{1,3,2,0:T(8,128)S(1)} fusion(f32[2,128,16,32]{1,3,2,0:T(8,128)S(1)} %copy-done.6, s32[]{:T(128)} %get-tuple-element.202, f32[16,32,32,32]{1,2,3,0:T(8,128)} %copy.39, f32[128,32,32]{0,1,2:T(8,128)S(1)} %get-tuple-element.220), kind=kOutput, calls=%fused_computation.14.clone.1 | convolution fusion | flops 805371904 | bytes 2883588 | tf_op jit(solution)/shard_map/while/body/eval_jaxpr/ijcd,sjd->sic/dot_general | solution.py:31
  208.7 39.1 %all-reduce.4.cloned.1.call-done = f32[1024,128]{1,0:T(8,128)} async-done(((f32[1024,128]{1,0:T(8,128)}), f32[1024,128]{1,0:T(8,128)}) %all-reduce.4.cloned.1.call-update) | async-done | bytes 524304 | tf_op jit(solution)/shard_map/psum | solution.py:63
  249.0 10.6 %psum.38 = f32[128]{0:T(128)S(1)} all-reduce(f32[128]{0:T(128)S(1)} %reduce_sum.9), channel_id=1, replica_groups=mesh['row'=8,'col'=4] {'col'}, use_global_device_ids=true, to_apply=%region_6.7 | all-reduce | flops 128 | bytes 1024 | tf_op jit(solution)/shard_map/psum | solution.py:63
  259.6 11.9 %psum.39 = f32[128]{0:T(128)S(1)} all-reduce(f32[128]{0:T(128)S(1)} %psum.38), channel_id=1, replica_groups=mesh['row'=8,'col'=4] {'row'}, use_global_device_ids=true, to_apply=%region_7.8 | all-reduce | flops 128 | bytes 1024 | tf_op jit(solution)/shard_map/psum | solution.py:64
  273.2 34.4 %all-reduce.6.cloned.1.call-done = (f32[128,32,32]{0,2,1:T(8,128)}, f32[1024,128]{1,0:T(8,128)}) async-done(((f32[128,32,32]{0,2,1:T(8,128)}, f32[1024,128]{1,0:T(8,128)}), (f32[128,32,32]{0,2,1:T(8,128)}, f32[1024,128]{1,0:T(8,128)})) %all-reduce.6.cloned.1.call-update) | async-done | bytes 1048592 | tf_op jit(solution)/shard_map/psum | solution.py:54
  (54 shorter events, 16.6 us)
Async XLA Ops:
  7.2 240.6 %all-reduce.4.cloned.1.call-start = ((), (), s32[]{:S(2)}) async-start(), calls=%async_computation | async-start | bytes 1048576 | tf_op jit(solution)/shard_map/psum | solution.py:63
  59.2 0.8 copy-start.2
  69.1 12.0 %copy-start.1 = (f32[1024,128]{1,0:T(8,128)S(1)}, f32[1024,128]{1,0:T(8,128)}, u32[]{:S(2)}) copy-start(f32[1024,128]{1,0:T(8,128)} %get-tuple-element.222) | copy-start | bytes 1572868 | tf_op jit(solution)/shard_map/while
  75.8 16.1 %copy-start.4 = (f32[128,32,32]{0,2,1:T(8,128)S(1)}, f32[128,32,32]{0,2,1:T(8,128)}, u32[]{:S(2)}) copy-start(f32[128,32,32]{0,2,1:T(8,128)} %get-tuple-element.204) | copy-start | bytes 1572868 | tf_op jit(solution)/shard_map/while
  81.1 28.7 %copy-start.8 = (f32[128]{0:T(128)S(1)}, f32[128]{0:T(128)}, u32[]{:S(2)}) copy-start(f32[128]{0:T(128)} %get-tuple-element.223) | copy-start | bytes 1540 | tf_op jit(solution)/shard_map/while
  88.7 3.2 %copy-start = (f32[16,32,32,32]{3,1,2,0:T(8,128)}, f32[16,32,32,32]{3,1,2,0:T(8,128)S(1)}, u32[]{:S(2)}) copy-start(f32[16,32,32,32]{3,1,2,0:T(8,128)S(1)} %fusion.68) | copy-start | bytes 6291460 | tf_op jit(solution)/shard_map/while
  108.9 0.8 copy-start.5
  112.2 10.6 %copy-start.6 = (f32[2,128,16,32]{1,3,2,0:T(8,128)S(1)}, f32[2,128,16,32]{1,3,2,0:T(8,128)}, u32[]{:S(2)}) copy-start(f32[2,128,16,32]{1,3,2,0:T(8,128)} %get-tuple-element.206) | copy-start | bytes 1572868 | tf_op jit(solution)/shard_map/while
  122.9 10.0 %copy-start.3 = (f32[2,128,16,32]{1,3,2,0:T(8,128)S(1)}, f32[2,128,16,32]{1,3,2,0:T(8,128)}, u32[]{:S(2)}) copy-start(f32[2,128,16,32]{1,3,2,0:T(8,128)} %copy-done.2) | copy-start | bytes 1572868 | tf_op jit(solution)/shard_map/while
  132.1 0.8 copy-start.7
  132.9 0.8 copy-start.2
  142.7 12.1 %copy-start.1 = (f32[1024,128]{1,0:T(8,128)S(1)}, f32[1024,128]{1,0:T(8,128)}, u32[]{:S(2)}) copy-start(f32[1024,128]{1,0:T(8,128)} %get-tuple-element.222) | copy-start | bytes 1572868 | tf_op jit(solution)/shard_map/while
  149.4 16.3 %copy-start.4 = (f32[128,32,32]{0,2,1:T(8,128)S(1)}, f32[128,32,32]{0,2,1:T(8,128)}, u32[]{:S(2)}) copy-start(f32[128,32,32]{0,2,1:T(8,128)} %get-tuple-element.204) | copy-start | bytes 1572868 | tf_op jit(solution)/shard_map/while
  154.9 28.7 %copy-start.8 = (f32[128]{0:T(128)S(1)}, f32[128]{0:T(128)}, u32[]{:S(2)}) copy-start(f32[128]{0:T(128)} %get-tuple-element.223) | copy-start | bytes 1540 | tf_op jit(solution)/shard_map/while
  162.5 3.2 %copy-start = (f32[16,32,32,32]{3,1,2,0:T(8,128)}, f32[16,32,32,32]{3,1,2,0:T(8,128)S(1)}, u32[]{:S(2)}) copy-start(f32[16,32,32,32]{3,1,2,0:T(8,128)S(1)} %fusion.68) | copy-start | bytes 6291460 | tf_op jit(solution)/shard_map/while
  182.7 0.8 copy-start.5
  186.0 10.6 %copy-start.6 = (f32[2,128,16,32]{1,3,2,0:T(8,128)S(1)}, f32[2,128,16,32]{1,3,2,0:T(8,128)}, u32[]{:S(2)}) copy-start(f32[2,128,16,32]{1,3,2,0:T(8,128)} %get-tuple-element.206) | copy-start | bytes 1572868 | tf_op jit(solution)/shard_map/while
  196.7 10.0 %copy-start.3 = (f32[2,128,16,32]{1,3,2,0:T(8,128)S(1)}, f32[2,128,16,32]{1,3,2,0:T(8,128)}, u32[]{:S(2)}) copy-start(f32[2,128,16,32]{1,3,2,0:T(8,128)} %copy-done.2) | copy-start | bytes 1572868 | tf_op jit(solution)/shard_map/while
  205.9 0.8 copy-start.7
  206.7 100.9 %all-reduce.6.cloned.1.call-start = ((), (), s32[]{:S(2)}) async-start(), calls=%async_computation.1 | async-start | bytes 2097152 | tf_op jit(solution)/shard_map/psum | solution.py:54
  206.8 64.7 %collective-permute-start = (f32[128,32,32]{0,2,1:T(8,128)}, f32[128,32,32]{0,2,1:T(8,128)S(1)}, u32[]{:S(2)}, u32[]{:S(2)}) collective-permute-start(f32[128,32,32]{0,2,1:T(8,128)} %bitcast.115), channel_id=1, source_target_pairs={{0,1},{1,0},{2,3},{3,2},{4,5},{5,4},{6,7},{7,6},{8,9},{9,8},{10,11... | collective-permute-start | bytes 1572872 | tf_op jit(solution)/shard_map/ppermute | solution.py:51
  272.6 38.4 %collective-permute-start.1 = (f32[128,32,32]{0,2,1:T(8,128)S(1)}, f32[128,32,32]{0,2,1:T(8,128)S(1)}, u32[]{:S(2)}, u32[]{:S(2)}) collective-permute-start(f32[128,32,32]{0,2,1:T(8,128)S(1)} %bitcast_add_fusion), channel_id=1, source_target_pairs={{0,2},{1,3},{2,0},{3,1},{4,6},{5,7},{6,4},{7,5},{8,10},{9,11},{10,... | collective-permute-start | bytes 1572872 | tf_op jit(solution)/shard_map/ppermute | solution.py:51
Sparse Core Ops, SparseCore 0:
  206.8 40.8 all-reduce.3
  251.0 56.5 all-reduce.5
